TPU v7x, 32 devices: a whole 2x2x4 slice. The times are simulated.
32 devices in a mesh: row: 4 (over y, x), col: 8 (over z, core).
Axes of the slice: x: 2, y: 2, z: 4, core: 2. Of those that a mesh axis runs over, the one named last changes fastest.
Arguments:
- stiffness: float32 [12, 4, 128, 6144], P(None, 'row', None, 'col'), may hold values from -8 to 8
- lower_first: float32 [1024, 10, 4, 128], P('col', None, 'row'), may hold values from -0.1875 to 0.1875
- lower_second: float32 [1024, 8, 4, 128], P('col', None, 'row'), may hold values from -0.1875 to 0.1875
- diag_inv: float32 [2, 1024, 2, 4, 128], P(None, 'col', None, 'row'), as said below
Outputs:
- reduced: float32 [12, 4, 128, 6144], P(None, 'row', None, 'col')
Inputs may be any that keep to these rules, and one draw needn't show every extreme that they name: Each block of diag_inv, read as a 1024 x 1024 matrix, is zero above its diagonal and has a positive diagonal.
All inputs are finite; a program needn't handle non-finite values.
Results may differ from a plain program's by a relative error of at most 0.000086.
Values sent between devices are 32-bit elements; how exact they have to be, the bound alone decides.
A program may use at most 128 MiB of HBM per device.

v0:
```python
import jax
import jax.numpy as jnp
from jax import lax
from jax.sharding import PartitionSpec as P


def product(left, right):
    return jnp.dot(left, right, precision=lax.Precision.HIGHEST, preferred_element_type=jnp.float32)


def apply_cols(columns, factor):
    return lax.dot_general(
        columns,
        factor,
        (((0,), (0,)), ((), ())),
        precision=lax.Precision.HIGHEST,
        preferred_element_type=jnp.float32,
    )


def shards(stiffness, lower_first, lower_second, diag_inv):
    cycles = stiffness.shape[0]
    rblk = stiffness.shape[2]
    cdev = stiffness.shape[3]
    pcount = diag_inv.shape[2]
    nrow = lax.axis_size("row")
    nb = diag_inv.shape[1] * lax.axis_size("col")
    height = pcount * rblk
    matrix_rows = stiffness.reshape(cycles * rblk, cdev)
    inv_cols = lax.all_gather(diag_inv, "col", axis=1, tiled=True)
    inverse = inv_cols.reshape(2, nb, height)

    def own_rows(solved):
        grouped = solved.reshape(pcount, nrow, rblk, cdev)
        mine = lax.dynamic_slice_in_dim(grouped, lax.axis_index("row"), 1, 1)
        return mine.reshape(height, cdev)

    w_first = lax.psum(product(inverse[0], matrix_rows[:height]), "row")
    coupling = lax.all_gather(lower_first[:, :pcount], "col", axis=0, tiled=True).reshape(
        nb, height
    )
    w_second = lax.psum(
        product(inverse[1], matrix_rows[height : 2 * height] - apply_cols(coupling, w_first)), "row"
    )
    pieces = (
        lax.all_gather(lower_first[:, pcount:], "col", axis=0, tiled=True),
        lax.all_gather(lower_second, "col", axis=0, tiled=True),
    )
    count = pieces[0].shape[0]
    first_piece = pieces[0].reshape(count, -1)
    second_piece = pieces[1].reshape(count, -1)
    remain = (
        matrix_rows[2 * height :]
        - apply_cols(first_piece, w_first)
        - apply_cols(second_piece, w_second)
    )
    stacked = jnp.concatenate([own_rows(w_first), own_rows(w_second), remain], axis=0)
    return stacked.reshape(cycles, 1, rblk, cdev)


def solution(mesh):
    placed = (
        P(None, "row", None, "col"),
        P("col", None, "row", None),
        P("col", None, "row", None),
        P(None, "col", None, "row", None),
    )
    return jax.shard_map(
        shards, mesh=mesh, in_specs=placed, out_specs=P(None, "row", None, "col"), check_vma=False
    )
```

profile of v0, /device:TPU:0, one launch (start us, length us, event | category | flops | bytes accessed | tf_op | source)
XLA Modules:
  0.0 378.0 jit_solution(10535140194078627687)
XLA Ops:
  6.5 0.7 all-gather.5.cloned.1.call-update
  7.3 0.0 all-gather.7.cloned.1.call-start
  7.3 1.6 slice.37
  8.9 0.0 all-reduce.3.cloned.1.call-start
  8.9 1.5 fusion.16
  10.4 30.4 %all-gather.5.cloned.1.call-done = f32[2,1024,2,1,128]{4,3,2,1,0:T(1,128)} async-done(((f32[2,128,2,1,128]{4,3,2,1,0:T(1,128)}), f32[2,1024,2,1,128]{4,3,2,1,0:T(1,128)}) %all-gather.5.cloned.1.call-update) | async-done | bytes 2097168 | tf_op jit(solution)/shard_map/all_gather | solution.py:30
  40.8 7.8 %slice_reduce_fusion = (f32[1024,2,128]{2,1,0:T(2,128)S(1)}, f32[1024,2,128]{2,1,0:T(2,128)S(1)}) fusion(f32[2,1024,2,1,128]{4,3,2,1,0:T(1,128)} %all-gather.5.cloned.1.call-done), kind=kLoop, calls=%fused_computation.19 | loop fusion | bytes 4194304 | tf_op jit(solution)/shard_map/slice | solution.py:43
  48.7 4.4 %fusion.13 = f32[1024,768]{1,0:T(8,128)} fusion(f32[256,768]{1,0:T(8,128)S(1)} %bitcast.71, f32[128,8,2,128]{3,2,1,0:T(2,128)S(1)} %bitcast.68), kind=kOutput, calls=%fused_computation.16 | convolution fusion | flops 2415919104 | bytes 4980736 | tf_op jit(solution)/shard_map/dot_general | solution.py:8
  53.1 0.2 all-reduce.5.cloned.1.call-start
  53.3 0.3 copy.21
  53.6 10.5 %all-gather.7.cloned.1.call-done = f32[1024,2,1,128]{3,1,2,0:T(2,128)} async-done(((f32[128,2,1,128]{3,1,2,0:T(2,128)}), f32[1024,2,1,128]{3,1,2,0:T(2,128)}) %all-gather.7.cloned.1.call-update) | async-done | bytes 1048592 | tf_op jit(solution)/shard_map/all_gather | solution.py:39
  64.1 89.7 %all-reduce.3.cloned.1.call-done = f32[1024,768]{1,0:T(8,128)} async-done(((f32[1024,768]{1,0:T(8,128)}), f32[1024,768]{1,0:T(8,128)}) %all-reduce.3.cloned.1.call-update) | async-done | bytes 3145744 | tf_op jit(solution)/shard_map/psum | solution.py:38
  153.8 7.2 %fusion.8 = f32[256,768]{0,1:T(8,128)S(1)} fusion(f32[256,768]{0,1:T(8,128)S(1)} %copy.21, f32[1024,768]{1,0:T(8,128)} %all-reduce.3.cloned.1.call-done, f32[128,8,2,128]{3,2,1,0:T(2,128)} %bitcast.76), kind=kOutput, calls=%fused_computation.11 | convolution fusion | flops 2416115712 | bytes 5767168 | tf_op jit(solution)/shard_map/dot_general | solution.py:12
  161.0 4.4 %convolution_bitcast_fusion = f32[1024,768]{0,1:T(8,128)} fusion(f32[256,768]{0,1:T(8,128)S(1)} %fusion.8, f32[128,8,2,128]{3,2,1,0:T(2,128)S(1)} %bitcast.67), kind=kOutput, calls=%fused_computation.9 | convolution fusion | flops 2415919104 | bytes 4980736 | tf_op jit(solution)/shard_map/dot_general | solution.py:8
  165.4 0.0 all-gather.11.cloned.1.call-start
  165.5 0.5 all-gather.11.cloned.1.call-update
  166.0 0.3 all-gather.9.cloned.1.call-start
  166.3 0.8 slice.41
  167.2 3.8 slice.39
  170.9 4.1 %copy.22 = f32[1024,768]{0,1:T(8,128)} copy(f32[1024,768]{1,0:T(8,128)} %bitcast.65) | data formatting | bytes 6291456 | tf_op jit(solution)/shard_map/slice | solution.py:53
  175.1 0.9 constant_dynamic-slice_fusion
  176.0 2.3 copy.20
  178.3 74.2 %all-reduce.5.cloned.1.call-done = f32[1024,768]{0,1:T(8,128)} async-done(((f32[1024,768]{0,1:T(8,128)}), f32[1024,768]{0,1:T(8,128)}) %all-reduce.5.cloned.1.call-update) | async-done | bytes 3145744 | tf_op jit(solution)/shard_map/psum | solution.py:42
  252.5 5.1 %reshape.36 = f32[2,4,128,768]{2,1,0,3:T(4,128)} reshape(f32[1024,768]{0,1:T(8,128)} %all-reduce.5.cloned.1.call-done) | data formatting | bytes 6291456 | tf_op jit(solution)/shard_map/reshape | solution.py:34
  257.7 4.6 %dynamic-slice_reduce_fusion = f32[2,128,768]{1,0,2:T(2,128)S(1)} fusion(f32[2,4,128,768]{2,1,0,3:T(4,128)} %reshape.36, s32[]{:T(128)S(6)} %select_n.4), kind=kLoop, calls=%fused_computation.22 | loop fusion | bytes 1572868 | tf_op jit(solution)/shard_map/dynamic_slice | solution.py:35
  262.2 0.9 copy.54
  263.2 37.7 %all-gather.11.cloned.1.call-done = f32[1024,8,1,128]{3,1,2,0:T(8,128)} async-done(((f32[128,8,1,128]{3,1,2,0:T(8,128)}), f32[1024,8,1,128]{3,1,2,0:T(8,128)}) %all-gather.11.cloned.1.call-update) | async-done | bytes 4194320 | tf_op jit(solution)/shard_map/all_gather | solution.py:47
  300.9 14.8 %fusion = f32[768,1024]{1,0:T(8,128)} fusion(f32[1024,768]{0,1:T(8,128)} %all-reduce.5.cloned.1.call-done, f32[128,8,8,128]{3,2,1,0:T(8,128)} %bitcast.66), kind=kOutput, calls=%fused_computation.1 | convolution fusion | flops 9663676416 | bytes 10485760 | tf_op jit(solution)/shard_map/dot_general | solution.py:12
  315.6 32.4 %all-gather.9.cloned.1.call-done = f32[1024,8,1,128]{3,1,2,0:T(8,128)} async-done(((f32[128,8,1,128]{3,1,2,0:T(8,128)}), f32[1024,8,1,128]{3,1,2,0:T(8,128)}) %all-gather.9.cloned.1.call-update) | async-done | bytes 4194320 | tf_op jit(solution)/shard_map/all_gather | solution.py:46
  348.0 14.4 %bitcast_subtract_fusion = f32[1024,768]{0,1:T(8,128)S(1)} fusion(f32[768,1024]{1,0:T(8,128)} %fusion, f32[1024,768]{0,1:T(8,128)} %copy.22, f32[1024,768]{1,0:T(8,128)S(1)} %copy-done, f32[128,8,8,128]{3,2,1,0:T(8,128)} %bitcast.69), kind=kOutput, calls=%fused_computation.7 | convolution fusion | flops 9665249280 | bytes 16777216 | tf_op jit(solution)/shard_map/dot_general | solution.py:12
  362.5 2.6 pad_maximum_fusion
  365.1 6.0 %copy.18 = f32[1536,768]{1,0:T(8,128)} copy(f32[1536,768]{0,1:T(8,128)} %pad_maximum_fusion) | data formatting | bytes 9437184 | tf_op jit(solution)/shard_map/concatenate | solution.py:57
  (13 shorter events, 0.1 us)
Async XLA Ops:
  6.5 34.3 %all-gather.5.cloned.1.call-start = ((), (), s32[]{:S(2)}) async-start(), calls=%async_computation | async-start | bytes 2359296 | tf_op jit(solution)/shard_map/all_gather | solution.py:30
  7.3 56.9 %all-gather.7.cloned.1.call-start = ((), (), s32[]{:S(2)}) async-start(), calls=%async_computation.2 | async-start | bytes 1179648 | tf_op jit(solution)/shard_map/all_gather | solution.py:39
  8.9 144.9 %all-reduce.3.cloned.1.call-start = ((), (), s32[]{:S(2)}) async-start(), calls=%async_computation.1 | async-start | bytes 6291456 | tf_op jit(solution)/shard_map/psum | solution.py:38
  53.1 199.4 %all-reduce.5.cloned.1.call-start = ((), (), s32[]{:S(2)}) async-start(), calls=%async_computation.3 | async-start | bytes 6291456 | tf_op jit(solution)/shard_map/psum | solution.py:42
  161.0 5.3 %copy-start.3 = (f32[128,10,1,128]{3,2,1,0:T(1,128)S(1)}, f32[128,10,1,128]{3,2,1,0:T(1,128)}, u32[]{:S(2)}) copy-start(f32[128,10,1,128]{3,2,1,0:T(1,128)} %param.5) | copy-start | bytes 1966084
  165.4 135.4 %all-gather.11.cloned.1.call-start = ((), (), s32[]{:S(2)}) async-start(), calls=%async_computation.5 | async-start | bytes 4718592 | tf_op jit(solution)/shard_map/all_gather | solution.py:47
  166.0 182.0 %all-gather.9.cloned.1.call-start = ((), (), s32[]{:S(2)}) async-start(), calls=%async_computation.4 | async-start | bytes 4718592 | tf_op jit(solution)/shard_map/all_gather | solution.py:46
  170.9 4.1 %copy-start = (f32[1024,768]{1,0:T(8,128)S(1)}, f32[1024,768]{1,0:T(8,128)}, u32[]{:S(2)}) copy-start(f32[1024,768]{1,0:T(8,128)} %all-reduce.3.cloned.1.call-done) | copy-start | bytes 9437188
  348.0 14.4 %copy-start.1 = (f32[256,768]{0,1:T(8,128)S(1)}, f32[256,768]{0,1:T(8,128)}, u32[]{:S(2)}) copy-start(f32[256,768]{0,1:T(8,128)} %copy.20) | copy-start | bytes 2359300
  348.0 14.4 %copy-start.2 = (f32[96,8,2,128]{3,1,2,0:T(8,128)S(1)}, f32[96,8,2,128]{3,1,2,0:T(8,128)}, u32[]{:S(2)}) copy-start(f32[96,8,2,128]{3,1,2,0:T(8,128)} %copy.54) | copy-start | bytes 2359300
Sparse Core Ops, SparseCore 0:
  8.9 31.8 all-gather.4
  42.4 21.6 all-gather.6
  67.2 86.5 all-reduce.2
  165.5 86.9 all-reduce.4
  254.0 46.8 all-gather.10
  302.3 45.6 all-gather.8
where the time goes:
time: 378 us
  waiting for transfers between devices  276 us (73%)
  matrix products  45.1 us (12%)
  local copies, waits for them, and re-layouts  39.8 us (11%)
  between operations  13.6 us (4%)
    psum x1, waiting for transfers between devices, shards(): w_first = lax.psum(product(inverse[0], matrix_rows[:height]), 'row')  89.7 us
    psum x1, waiting for transfers between devices, shards(): lax.psum(product(inverse[1], matrix_rows[height:2 * height] - apply_cols(...  74.2 us
    all_gather x1, waiting for transfers between devices, shards(): lax.all_gather(lower_second, 'col', axis=0, tiled=True)  37.7 us
    dot_general x3, matrix products, apply_cols(): lax.dot_general(columns, factor, (((0,), (0,)), ((), ())), precision=lax....  36.4 us
    all_gather x1, waiting for transfers between devices, shards(): lax.all_gather(lower_first[:, pcount:], 'col', axis=0, tiled=True)  32.4 us
    all_gather x1, waiting for transfers between devices, shards(): inv_cols = lax.all_gather(diag_inv, 'col', axis=1, tiled=True)  30.4 us
    all_gather x1, waiting for transfers between devices, shards(): lax.all_gather(lower_first[:, :pcount], 'col', axis=0, tiled=True)  10.5 us
    dot_general x2, matrix products, product(): jnp.dot(left, right, precision=lax.Precision.HIGHEST, preferred_element_t...  8.73 us
  transfers between devices with their start and end apart: 6, of which 6 were waited for; matrix products, arithmetic and copies ran while one was open for 14% of the time, Pallas kernels for 0%

commit v1 on v0

--- a/solution.py
+++ b/solution.py
@@ -2,6 +2,16 @@
 import jax.numpy as jnp
 from jax import lax
 from jax.sharding import PartitionSpec as P
+
+
+def pass_along(value, axis, d):
+    peers = lax.axis_size(axis)
+    moving, blocks = (value, [value])
+    for _ in range(peers - 1):
+        moving = lax.ppermute(moving, axis, [(i, (i + 1) % peers) for i in range(peers)])
+        blocks.insert(0, moving)
+    flat = jnp.concatenate(blocks, axis=d)
+    return jnp.roll(flat, (lax.axis_index(axis) + 1) * value.shape[d], axis=d)
 
 
 def product(left, right):
@@ -27,7 +37,7 @@
     nb = diag_inv.shape[1] * lax.axis_size("col")
     height = pcount * rblk
     matrix_rows = stiffness.reshape(cycles * rblk, cdev)
-    inv_cols = lax.all_gather(diag_inv, "col", axis=1, tiled=True)
+    inv_cols = pass_along(diag_inv, "col", 1)
     inverse = inv_cols.reshape(2, nb, height)
 
     def own_rows(solved):

time: 378 us -> 311 us (0.82)
  waiting for transfers between devices: 276 us -> 211 us
  local copies, waits for them, and re-layouts: 39.8 us -> 35.6 us
    ppermute x0 -> x7, waiting for transfers between devices: none -> 50.9 us  [pass_along(): lax.ppermute(moving, axis, [(i, (i + 1) % peers) for i in range(peers)])]
    all_gather x1, waiting for transfers between devices: 37.7 us -> 0.01 us  [shards(): lax.all_gather(lower_second, 'col', axis=0, tiled=True)]
    all_gather x1, waiting for transfers between devices: 32.4 us -> 0.01 us  [shards(): lax.all_gather(lower_first[:, pcount:], 'col', axis=0, tiled=True)]
    all_gather x1 -> x0, waiting for transfers between devices: 30.4 us -> none  [shards(): inv_cols = lax.all_gather(diag_inv, 'col', axis=1, tiled=True)]
    all_gather x1, waiting for transfers between devices: 10.5 us -> 0.02 us  [shards(): lax.all_gather(lower_first[:, :pcount], 'col', axis=0, tiled=True)]
    reshape x1 -> x0, local copies, waits for them, and re-layouts: 5.13 us -> none  [own_rows(): grouped = solved.reshape(pcount, nrow, rblk, cdev)]
    psum x1, waiting for transfers between devices: 89.7 us -> 85.5 us  [shards(): w_first = lax.psum(product(inverse[0], matrix_rows[:height]), 'row')]
  transfers between devices with their start and end apart: 6 -> 12, of which waited for: 6 -> 9; matrix products, arithmetic and copies ran while one was open for 14% -> 16% of each run, Pallas kernels for 0% -> 0%
where the time goes in v1:
time: 311 us; the launch traced here: 310 us
  waiting for transfers between devices  211 us (68%)
  matrix products  45.5 us (15%)
  local copies, waits for them, and re-layouts  35.6 us (11%)
  between operations  14.8 us (5%)
    psum x1, waiting for transfers between devices, shards(): w_first = lax.psum(product(inverse[0], matrix_rows[:height]), 'row')  85.5 us
    psum x1, waiting for transfers between devices, shards(): lax.psum(product(inverse[1], matrix_rows[height:2 * height] - apply_cols(...  73.6 us
    ppermute x7, waiting for transfers between devices, pass_along(): lax.ppermute(moving, axis, [(i, (i + 1) % peers) for i in range(peers)])  50.9 us
    dot_general x3, matrix products, apply_cols(): lax.dot_general(columns, factor, (((0,), (0,)), ((), ())), precision=lax....  36.6 us
    dot_general x2, matrix products, product(): jnp.dot(left, right, precision=lax.Precision.HIGHEST, preferred_element_t...  8.94 us
    slice x2, local copies, waits for them, and re-layouts, shards(): matrix_rows[2 * height:] - apply_cols(first_piece, w_first)  7.9 us
    slice x1, local copies, waits for them, and re-layouts, shards(): inverse[1]  6.61 us
  transfers between devices with their start and end apart: 12, of which 9 were waited for; matrix products, arithmetic and copies ran while one was open for 16% of the time, Pallas kernels for 0%

profile of v1, /device:TPU:0, one launch (start us, length us, event | category | flops | bytes accessed | tf_op | source)
XLA Modules:
  0.0 310.3 jit_solution(14289034947705757908)
XLA Ops:
  7.4 0.5 collective-permute-start
  7.9 8.4 %collective-permute-done = f32[2,128,2,1,128]{4,3,2,1,0:T(1,128)S(1)} collective-permute-done((f32[2,128,2,1,128]{4,3,2,1,0:T(1,128)}, f32[2,128,2,1,128]{4,3,2,1,0:T(1,128)S(1)}, u32[]{:S(2)}, u32[]{:S(2)}) %collective-permute-start) | collective-permute-done | bytes 262176 | tf_op jit(solution)/shard_map/ppermute | solution.py:11
  16.2 7.6 %collective-permute-done.1 = f32[2,128,2,1,128]{4,3,2,1,0:T(1,128)S(1)} collective-permute-done((f32[2,128,2,1,128]{4,3,2,1,0:T(1,128)S(1)}, f32[2,128,2,1,128]{4,3,2,1,0:T(1,128)S(1)}, u32[]{:S(2)}, u32[]{:S(2)}) %collective-permute-start.1) | collective-permute-done | bytes 262176 | tf_op jit(solution)/shard_map/ppermute | solution.py:11
  23.8 7.6 %collective-permute-done.2 = f32[2,128,2,1,128]{4,3,2,1,0:T(1,128)S(1)} collective-permute-done((f32[2,128,2,1,128]{4,3,2,1,0:T(1,128)S(1)}, f32[2,128,2,1,128]{4,3,2,1,0:T(1,128)S(1)}, u32[]{:S(2)}, u32[]{:S(2)}) %collective-permute-start.2) | collective-permute-done | bytes 262176 | tf_op jit(solution)/shard_map/ppermute | solution.py:11
  31.4 7.6 %collective-permute-done.3 = f32[2,128,2,1,128]{4,3,2,1,0:T(1,128)S(1)} collective-permute-done((f32[2,128,2,1,128]{4,3,2,1,0:T(1,128)S(1)}, f32[2,128,2,1,128]{4,3,2,1,0:T(1,128)S(1)}, u32[]{:S(2)}, u32[]{:S(2)}) %collective-permute-start.3) | collective-permute-done | bytes 262176 | tf_op jit(solution)/shard_map/ppermute | solution.py:11
  39.0 7.6 %collective-permute-done.4 = f32[2,128,2,1,128]{4,3,2,1,0:T(1,128)S(1)} collective-permute-done((f32[2,128,2,1,128]{4,3,2,1,0:T(1,128)S(1)}, f32[2,128,2,1,128]{4,3,2,1,0:T(1,128)S(1)}, u32[]{:S(2)}, u32[]{:S(2)}) %collective-permute-start.4) | collective-permute-done | bytes 262176 | tf_op jit(solution)/shard_map/ppermute | solution.py:11
  46.6 1.6 slice.38
  48.3 5.9 %collective-permute-done.5 = f32[2,128,2,1,128]{4,3,2,1,0:T(1,128)S(1)} collective-permute-done((f32[2,128,2,1,128]{4,3,2,1,0:T(1,128)S(1)}, f32[2,128,2,1,128]{4,3,2,1,0:T(1,128)S(1)}, u32[]{:S(2)}, u32[]{:S(2)}) %collective-permute-start.5) | collective-permute-done | bytes 262176 | tf_op jit(solution)/shard_map/ppermute | solution.py:11
  54.2 1.5 fusion.17
  55.7 6.3 %collective-permute-done.6 = f32[2,128,2,1,128]{4,3,2,1,0:T(1,128)S(1)} collective-permute-done((f32[2,128,2,1,128]{4,3,2,1,0:T(1,128)S(1)}, f32[2,128,2,1,128]{4,3,2,1,0:T(1,128)S(1)}, u32[]{:S(2)}, u32[]{:S(2)}) %collective-permute-start.6) | collective-permute-done | bytes 262176 | tf_op jit(solution)/shard_map/ppermute | solution.py:11
  62.2 0.2 constant_dynamic-update-slice_fusion.14
  63.6 0.2 constant_dynamic-update-slice_fusion.7
  65.3 6.6 %dynamic-slice_reduce_fusion = (f32[1024,2,128]{2,1,0:T(2,128)S(1)}, f32[1024,2,128]{2,1,0:T(2,128)S(1)}) fusion(f32[2,2048,2,1,128]{4,3,2,1,0:T(1,128)S(1)} %constant_dynamic-update-slice_fusion, s32[]{:T(128)S(6)} %add.29, s32[]{:T(128)S(6)} %select_n.18), kind=kLoop, calls=%fused_computation.19 | loop fusion | bytes 4194312 | tf_op jit(solution)/shard_map/slice | solution.py:53
  71.9 4.6 %fusion.14 = f32[1024,768]{1,0:T(8,128)} fusion(f32[256,768]{1,0:T(8,128)S(1)} %bitcast.61, f32[128,8,2,128]{3,2,1,0:T(2,128)S(1)} %bitcast.59), kind=kOutput, calls=%fused_computation.16 | convolution fusion | flops 2415919104 | bytes 4980736 | tf_op jit(solution)/shard_map/dot_general | solution.py:18
  76.5 0.3 copy.24
  76.8 85.5 %all-reduce.3.cloned.1.call-done = f32[1024,768]{1,0:T(8,128)} async-done(((f32[1024,768]{1,0:T(8,128)}), f32[1024,768]{1,0:T(8,128)}) %all-reduce.3.cloned.1.call-update) | async-done | bytes 3145744 | tf_op jit(solution)/shard_map/psum | solution.py:48
  162.3 7.2 %fusion.8 = f32[256,768]{0,1:T(8,128)S(1)} fusion(f32[256,768]{0,1:T(8,128)S(1)} %copy.24, f32[1024,768]{1,0:T(8,128)} %all-reduce.3.cloned.1.call-done, f32[128,8,2,128]{3,2,1,0:T(2,128)} %bitcast.66), kind=kOutput, calls=%fused_computation.10 | convolution fusion | flops 2416115712 | bytes 5767168 | tf_op jit(solution)/shard_map/dot_general | solution.py:22
  169.6 4.4 %fusion.11 = f32[1024,768]{1,0:T(8,128)} fusion(f32[256,768]{0,1:T(8,128)S(1)} %fusion.8, f32[128,8,2,128]{3,2,1,0:T(2,128)S(1)} %bitcast.58), kind=kOutput, calls=%fused_computation.13 | convolution fusion | flops 2415919104 | bytes 4980736 | tf_op jit(solution)/shard_map/dot_general | solution.py:18
  174.0 0.7 all-gather.8.cloned.1.call-update
  174.7 0.3 all-gather.6.cloned.1.call-start
  175.0 0.8 slice.41
  175.8 3.8 %slice.39 = f32[8,1,128,768]{3,2,1,0:T(8,128)} slice(f32[12,1,128,768]{3,2,1,0:T(8,128)} %param.4), slice={[4:12], [0:1], [0:128], [0:768]} | slice | bytes 6291456 | tf_op jit(solution)/shard_map/slice | solution.py:63
  179.6 4.1 %copy.26 = f32[1024,768]{0,1:T(8,128)} copy(f32[1024,768]{1,0:T(8,128)} %bitcast.57) | data formatting | bytes 6291456 | tf_op jit(solution)/shard_map/slice | solution.py:63
  183.8 1.0 constant_dynamic-slice_fusion.1
  184.7 2.4 copy.23
  187.1 73.6 %all-reduce.5.cloned.1.call-done = f32[1024,768]{1,0:T(8,128)} async-done(((f32[1024,768]{1,0:T(8,128)}), f32[1024,768]{1,0:T(8,128)}) %all-reduce.5.cloned.1.call-update) | async-done | bytes 3145744 | tf_op jit(solution)/shard_map/psum | solution.py:52
  260.7 2.1 constant_dynamic-slice_fusion
  262.8 2.3 copy.25
  265.1 14.7 %fusion = f32[768,1024]{1,0:T(8,128)} fusion(f32[1024,768]{1,0:T(8,128)} %all-reduce.5.cloned.1.call-done, f32[128,8,8,128]{3,2,1,0:T(8,128)} %bitcast.70), kind=kOutput, calls=%fused_computation.1 | convolution fusion | flops 9663676416 | bytes 10485760 | tf_op jit(solution)/shard_map/dot_general | solution.py:22
  279.8 14.7 %bitcast_subtract_fusion = f32[1024,768]{0,1:T(8,128)S(1)} fusion(f32[768,1024]{1,0:T(8,128)} %fusion, f32[1024,768]{0,1:T(8,128)} %copy.26, f32[1024,768]{1,0:T(8,128)S(1)} %copy-done, f32[128,8,8,128]{3,2,1,0:T(8,128)} %bitcast.60), kind=kOutput, calls=%fused_computation.7 | convolution fusion | flops 9665249280 | bytes 16777216 | tf_op jit(solution)/shard_map/dot_general | solution.py:22
  294.5 2.6 pad_maximum_fusion
  297.1 6.0 %copy.21 = f32[1536,768]{1,0:T(8,128)} copy(f32[1536,768]{0,1:T(8,128)} %pad_maximum_fusion) | data formatting | bytes 9437184 | tf_op jit(solution)/shard_map/concatenate | solution.py:67
  (41 shorter events, 3.0 us)
Async XLA Ops:
  7.4 56.0 %copy-start.3 = (f32[2,128,2,1,128]{4,3,2,1,0:T(1,128)S(1)}, f32[2,128,2,1,128]{4,3,2,1,0:T(1,128)}, u32[]{:S(2)}) copy-start(f32[2,128,2,1,128]{4,3,2,1,0:T(1,128)} %param.7) | copy-start | bytes 786436
  7.4 69.4 %all-gather.4.cloned.1.call-start = ((), (), s32[]{:S(2)}) async-start(), calls=%async_computation.1 | async-start | bytes 1179648 | tf_op jit(solution)/shard_map/all_gather | solution.py:49
  7.4 8.8 %collective-permute-start = (f32[2,128,2,1,128]{4,3,2,1,0:T(1,128)}, f32[2,128,2,1,128]{4,3,2,1,0:T(1,128)S(1)}, u32[]{:S(2)}, u32[]{:S(2)}) collective-permute-start(f32[2,128,2,1,128]{4,3,2,1,0:T(1,128)} %param.7), channel_id=1, source_target_pairs={{0,1},{1,2},{2,3},{3,4},{4,5},{5,6},{6,7},{7,0},{8,9},{9,10},{10,1... | collective-permute-start | bytes 786440 | tf_op jit(solution)/shard_map/ppermute | solution.py:11
  16.2 7.6 %collective-permute-start.1 = (f32[2,128,2,1,128]{4,3,2,1,0:T(1,128)S(1)}, f32[2,128,2,1,128]{4,3,2,1,0:T(1,128)S(1)}, u32[]{:S(2)}, u32[]{:S(2)}) collective-permute-start(f32[2,128,2,1,128]{4,3,2,1,0:T(1,128)S(1)} %collective-permute-done), channel_id=1, source_target_pairs={{0,1},{1,2},{2,3},{3,4},{4,5},{5,6},{6,7},{7,0},{8,9},{9,10},{10,1... | collective-permute-start | bytes 786440 | tf_op jit(solution)/shard_map/ppermute | solution.py:11
  23.8 7.6 %collective-permute-start.2 = (f32[2,128,2,1,128]{4,3,2,1,0:T(1,128)S(1)}, f32[2,128,2,1,128]{4,3,2,1,0:T(1,128)S(1)}, u32[]{:S(2)}, u32[]{:S(2)}) collective-permute-start(f32[2,128,2,1,128]{4,3,2,1,0:T(1,128)S(1)} %collective-permute-done.1), channel_id=1, source_target_pairs={{0,1},{1,2},{2,3},{3,4},{4,5},{5,6},{6,7},{7,0},{8,9},{9,10},{10,1... | collective-permute-start | bytes 786440 | tf_op jit(solution)/shard_map/ppermute | solution.py:11
  31.4 7.6 %collective-permute-start.3 = (f32[2,128,2,1,128]{4,3,2,1,0:T(1,128)S(1)}, f32[2,128,2,1,128]{4,3,2,1,0:T(1,128)S(1)}, u32[]{:S(2)}, u32[]{:S(2)}) collective-permute-start(f32[2,128,2,1,128]{4,3,2,1,0:T(1,128)S(1)} %collective-permute-done.2), channel_id=1, source_target_pairs={{0,1},{1,2},{2,3},{3,4},{4,5},{5,6},{6,7},{7,0},{8,9},{9,10},{10,1... | collective-permute-start | bytes 786440 | tf_op jit(solution)/shard_map/ppermute | solution.py:11
  39.0 7.6 %collective-permute-start.4 = (f32[2,128,2,1,128]{4,3,2,1,0:T(1,128)S(1)}, f32[2,128,2,1,128]{4,3,2,1,0:T(1,128)S(1)}, u32[]{:S(2)}, u32[]{:S(2)}) collective-permute-start(f32[2,128,2,1,128]{4,3,2,1,0:T(1,128)S(1)} %collective-permute-done.3), channel_id=1, source_target_pairs={{0,1},{1,2},{2,3},{3,4},{4,5},{5,6},{6,7},{7,0},{8,9},{9,10},{10,1... | collective-permute-start | bytes 786440 | tf_op jit(solution)/shard_map/ppermute | solution.py:11
  46.6 7.6 %collective-permute-start.5 = (f32[2,128,2,1,128]{4,3,2,1,0:T(1,128)S(1)}, f32[2,128,2,1,128]{4,3,2,1,0:T(1,128)S(1)}, u32[]{:S(2)}, u32[]{:S(2)}) collective-permute-start(f32[2,128,2,1,128]{4,3,2,1,0:T(1,128)S(1)} %collective-permute-done.4), channel_id=1, source_target_pairs={{0,1},{1,2},{2,3},{3,4},{4,5},{5,6},{6,7},{7,0},{8,9},{9,10},{10,1... | collective-permute-start | bytes 786440 | tf_op jit(solution)/shard_map/ppermute | solution.py:11
  48.2 114.1 %all-reduce.3.cloned.1.call-start = ((), (), s32[]{:S(2)}) async-start(), calls=%async_computation | async-start | bytes 6291456 | tf_op jit(solution)/shard_map/psum | solution.py:48
  54.2 7.8 %collective-permute-start.6 = (f32[2,128,2,1,128]{4,3,2,1,0:T(1,128)S(1)}, f32[2,128,2,1,128]{4,3,2,1,0:T(1,128)S(1)}, u32[]{:S(2)}, u32[]{:S(2)}) collective-permute-start(f32[2,128,2,1,128]{4,3,2,1,0:T(1,128)S(1)} %collective-permute-done.5), channel_id=1, source_target_pairs={{0,1},{1,2},{2,3},{3,4},{4,5},{5,6},{6,7},{7,0},{8,9},{9,10},{10,1... | collective-permute-start | bytes 786440 | tf_op jit(solution)/shard_map/ppermute | solution.py:11
  76.5 184.3 %all-reduce.5.cloned.1.call-start = ((), (), s32[]{:S(2)}) async-start(), calls=%async_computation.2 | async-start | bytes 6291456 | tf_op jit(solution)/shard_map/psum | solution.py:52
  169.6 5.4 %copy-start.4 = (f32[128,10,1,128]{3,2,1,0:T(1,128)S(1)}, f32[128,10,1,128]{3,2,1,0:T(1,128)}, u32[]{:S(2)}) copy-start(f32[128,10,1,128]{3,2,1,0:T(1,128)} %param.5) | copy-start | bytes 1966084
  174.0 91.1 %all-gather.8.cloned.1.call-start = ((), (), s32[]{:S(2)}) async-start(), calls=%async_computation.4 | async-start | bytes 4718592 | tf_op jit(solution)/shard_map/all_gather | solution.py:57
  174.7 105.0 %all-gather.6.cloned.1.call-start = ((), (), s32[]{:S(2)}) async-start(), calls=%async_computation.3 | async-start | bytes 4718592 | tf_op jit(solution)/shard_map/all_gather | solution.py:56
  179.6 4.1 %copy-start = (f32[1024,768]{1,0:T(8,128)S(1)}, f32[1024,768]{1,0:T(8,128)}, u32[]{:S(2)}) copy-start(f32[1024,768]{1,0:T(8,128)} %all-reduce.3.cloned.1.call-done) | copy-start | bytes 9437188
  279.8 14.7 %copy-start.1 = (f32[256,768]{0,1:T(8,128)S(1)}, f32[256,768]{0,1:T(8,128)}, u32[]{:S(2)}) copy-start(f32[256,768]{0,1:T(8,128)} %copy.23) | copy-start | bytes 2359300
  279.8 14.7 %copy-start.2 = (f32[256,768]{0,1:T(8,128)S(1)}, f32[256,768]{0,1:T(8,128)}, u32[]{:S(2)}) copy-start(f32[256,768]{0,1:T(8,128)} %copy.25) | copy-start | bytes 2359300
Sparse Core Ops, SparseCore 0:
  48.3 24.7 all-gather.3
  176.4 46.8 all-gather.7
  224.9 45.6 all-gather.5
Sparse Core Ops, SparseCore 1:
  76.6 85.7 all-reduce.2
  174.0 86.6 all-reduce.4
